TPU v7x, 32 devices: a whole 2x2x4 slice. The times are simulated.
32 devices in a mesh: fsdp: 8 (over z, x), rep: 4 (over y, core).
Axes of the slice: x: 2, y: 2, z: 4, core: 2. Of those that a mesh axis runs over, the one named last changes fastest.
Arguments:
- tokens_x: bfloat16 [4096, 8192], P(('fsdp', 'rep')), may hold values from -6 to 6
- cotangent: bfloat16 [4096, 128], P(('fsdp', 'rep')), may hold values from -1 to 1
- master_weight: float32 [8192, 128], P('fsdp'), may hold values from -0.015625 to 0.015625
- first_moment: float32 [8192, 128], P('fsdp'), may hold values from -6 to 6
- second_moment: float32 [8192, 128], P('fsdp'), may hold values from 0.5 to 2
- hidden_dec: bfloat16 [2, 64, 8192], P(None, ('fsdp', 'rep')), may hold values from -6 to 6
- queries: bfloat16 [2, 64, 1024], P(None, ('fsdp', 'rep')), may hold values from -64 to 64
- new_values: bfloat16 [2, 64, 128], P(None, ('fsdp', 'rep')), may hold values from -6 to 6
- key_cache: bfloat16 [64, 1024, 128], P(('fsdp', 'rep')), may hold values from -64 to 64
- value_cache: bfloat16 [64, 1024, 128], P(('fsdp', 'rep')), may hold values from -6 to 6
- cache_lengths: int32 [64], P(('fsdp', 'rep')), may hold values from 2 to 1022, as said below
Outputs:
- weight_next: float32 [8192, 128], P('fsdp')
- first_next: float32 [8192, 128], P('fsdp')
- second_next: float32 [8192, 128], P('fsdp')
- rollout_weight: bfloat16 [8192, 128], replicated
- fresh_keys: bfloat16 [2, 64, 128], P(None, ('fsdp', 'rep'))
- attended: bfloat16 [2, 64, 1024], P(None, ('fsdp', 'rep'))
Inputs may be any that keep to these rules, and one draw needn't show every extreme that they name: `cache_lengths`: some row has exactly 1022 filled slots.
All inputs are finite; a program needn't handle non-finite values. Where the computation divides by a largest or mean magnitude, that divisor is 1e-20 or more.
Results may differ from a plain program's by a relative error of at most 0.0049.
Values may be sent and summed in bfloat16 or wider, within the bound.
A program may use at most 64 MiB of HBM per device.

v0:
```python
import math

import jax
import jax.numpy as jnp
from jax import lax
from jax.sharding import PartitionSpec as P

D = 8192
BLOCK = 128


beta_one = 0.9
beta_two = 0.95
adam_eps = 1e-08
learn_rate = 0.0003
weight_decay = 0.1
step_count = 100
rope_theta = 1000000.0
peak_eps = 1e-06


def adamw(weight, first, second, gradient):
    first_new = beta_one * first + (1.0 - beta_one) * gradient
    second_new = beta_two * second + (1.0 - beta_two) * gradient * gradient
    first_hat = first_new / (1.0 - beta_one**step_count)
    second_hat = second_new / (1.0 - beta_two**step_count)
    weight_new = weight - learn_rate * (
        first_hat / (jnp.sqrt(second_hat) + adam_eps) + weight_decay * weight
    )
    return (weight_new, first_new, second_new)


def rotate(values, positions):
    half = values.shape[-1] // 2
    freq = rope_theta ** (-jnp.arange(half, dtype=jnp.float32) * 2.0 / values.shape[-1])
    angle = positions.astype(jnp.float32)[..., None] * freq
    cosine = jnp.cos(angle)
    sine = jnp.sin(angle)
    first_half = values[..., :half]
    second_half = values[..., half:]
    return jnp.concatenate(
        [first_half * cosine - second_half * sine, second_half * cosine + first_half * sine],
        axis=-1,
    )


def project_keys(hidden_size, quantized_weight, scales, lengths):
    decode_step_count, row_count, block_width = hidden_size.shape
    block_count = scales.shape[0]
    part_count = jnp.einsum(
        "qht,hti->qhi",
        hidden_size.reshape(decode_step_count * row_count, block_count, block_width // block_count),
        quantized_weight.reshape(block_count, block_width // block_count, -1),
        preferred_element_type=jnp.float32,
    )
    raw = jnp.sum(part_count * scales[None, :, None], axis=1).reshape(
        decode_step_count, row_count, -1
    )
    positions = lengths[None, :] + jnp.arange(decode_step_count, dtype=jnp.int32)[:, None]
    return rotate(raw, positions).astype(jnp.bfloat16)


def attend(query, cache_keys, cache_values, fresh, fresh_values, lengths):
    decode_step_count, row_count, joined = query.shape
    head_dim = cache_keys.shape[-1]
    heads = joined // head_dim
    valid = jnp.arange(cache_keys.shape[1], dtype=jnp.int32)[None, None, :] < lengths[:, None, None]
    outputs = []
    for section_index in range(decode_step_count):
        query_now = query[section_index].reshape(row_count, heads, head_dim)
        scores_c = jnp.einsum(
            "rhd,rcd->rhc", query_now, cache_keys, preferred_element_type=jnp.float32
        ) / math.sqrt(head_dim)
        scores_f = jnp.einsum(
            "rhd,trd->rht", query_now, fresh, preferred_element_type=jnp.float32
        ) / math.sqrt(head_dim)
        scores_c = jnp.where(valid, scores_c, -jnp.inf)
        scores_f = jnp.where(
            (jnp.arange(decode_step_count) <= section_index)[None, None, :], scores_f, -jnp.inf
        )
        peak = jnp.maximum(jnp.max(scores_c, axis=2), jnp.max(scores_f, axis=2))[:, :, None]
        exp_c = jnp.exp(scores_c - peak)
        exp_f = jnp.exp(scores_f - peak)
        total = jnp.sum(exp_c, axis=2, keepdims=True) + jnp.sum(exp_f, axis=2, keepdims=True)
        prob_c = (exp_c / total).astype(jnp.bfloat16)
        prob_f = (exp_f / total).astype(jnp.bfloat16)
        mixed = jnp.einsum("rhc,rcd->rhd", prob_c, cache_values, preferred_element_type=jnp.float32)
        mixed = mixed + jnp.einsum(
            "rht,trd->rhd", prob_f, fresh_values, preferred_element_type=jnp.float32
        )
        outputs.append(mixed.reshape(row_count, joined).astype(jnp.bfloat16))
    return jnp.stack(outputs)


def shards(
    tokens_x,
    cotangent,
    master_weight,
    first_moment,
    second_moment,
    hidden_dec,
    queries,
    new_values,
    key_cache,
    value_cache,
    cache_lengths,
):
    shard_rows = master_weight.shape[0]
    partial_grad = lax.psum_scatter(
        lax.dot_general(
            tokens_x, cotangent, (((0,), (0,)), ((), ())), preferred_element_type=jnp.float32
        ),
        "fsdp",
        scatter_dimension=0,
        tiled=True,
    )
    gradient = lax.psum(partial_grad, "rep")
    weight_next, first_next, second_next = adamw(
        master_weight, first_moment, second_moment, gradient
    )
    block_count = D // BLOCK
    row_ids = lax.axis_index("fsdp") * shard_rows + jnp.arange(shard_rows, dtype=jnp.int32)
    member = (row_ids // BLOCK)[:, None] == jnp.arange(block_count, dtype=jnp.int32)[None, :]
    row_peak = jnp.max(jnp.abs(weight_next), axis=1)
    local_peaks = jnp.max(jnp.where(member, row_peak[:, None], 0.0), axis=0)
    scales = lax.pmax(local_peaks, "fsdp") + peak_eps
    row_scale = jnp.sum(jnp.where(member, scales[None, :], 0.0), axis=1)
    local_quant = (weight_next / row_scale[:, None]).astype(jnp.bfloat16)
    rollout_weight = lax.all_gather(local_quant, "fsdp", axis=0, tiled=True)
    fresh_keys = project_keys(hidden_dec, rollout_weight, scales, cache_lengths)
    attended = attend(queries, key_cache, value_cache, fresh_keys, new_values, cache_lengths)
    return (weight_next, first_next, second_next, rollout_weight, fresh_keys, attended)


def solution(mesh):
    return jax.shard_map(
        shards,
        mesh=mesh,
        in_specs=(
            P(("fsdp", "rep"), None),
            P(("fsdp", "rep"), None),
            P("fsdp", None),
            P("fsdp", None),
            P("fsdp", None),
            P(None, ("fsdp", "rep"), None),
            P(None, ("fsdp", "rep"), None),
            P(None, ("fsdp", "rep"), None),
            P(("fsdp", "rep"), None, None),
            P(("fsdp", "rep"), None, None),
            P(("fsdp", "rep")),
        ),
        out_specs=(
            P("fsdp", None),
            P("fsdp", None),
            P("fsdp", None),
            P(),
            P(None, ("fsdp", "rep"), None),
            P(None, ("fsdp", "rep"), None),
        ),
        check_vma=False,
    )
```

profile of v0, /device:TPU:0, one launch (start us, length us, event | category | flops | bytes accessed | tf_op | source)
XLA Modules:
  0.0 224.9 jit_solution(2394929650028422589)
XLA Ops:
  7.2 1.5 copy-done
  8.8 3.4 %fusion.52 = f32[8192,128]{1,0:T(8,128)} fusion(bf16[128,8192]{1,0:T(8,128)(2,1)S(1)} %copy-done, bf16[128,128]{1,0:T(8,128)(2,1)} %param.12), kind=kOutput, calls=%fused_computation.92 | convolution fusion | flops 268435456 | bytes 6324224 | tf_op jit(solution)/shard_map/dot_general | solution.py:110
  12.2 0.0 all-reduce.2.cloned.1.call-start
  12.3 91.1 %reduce-scatter.2.cloned.1.call-done = f32[1024,128]{1,0:T(8,128)} async-done(((f32[8192,128]{1,0:T(8,128)}), f32[1024,128]{1,0:T(8,128)}) %reduce-scatter.2.cloned.1.call-update) | async-done | bytes 524304 | tf_op jit(solution)/shard_map/reduce_scatter | solution.py:109
  103.4 0.0 all-gather.2.cloned.1.call-start
  103.6 35.3 %all-reduce.2.cloned.1.call-done = f32[1024,128]{1,0:T(8,128)} async-done(((f32[1024,128]{1,0:T(8,128)}), f32[1024,128]{1,0:T(8,128)}) %all-reduce.2.cloned.1.call-update) | async-done | bytes 524304 | tf_op jit(solution)/shard_map/psum | solution.py:117
  138.8 2.9 %abs_reduce_fusion = (f32[1024]{0:T(1024)S(1)}, f32[1024,128]{1,0:T(8,128)S(1)}, f32[1024,128]{1,0:T(8,128)}, f32[1024,128]{1,0:T(8,128)}) fusion(f32[1024,128]{1,0:T(8,128)} %param.13, f32[1024,128]{1,0:T(8,128)} %all-reduce.2.cloned.1.call-done, f32[1024,128]{1,0:T(8,128)} %param.14, f32[1024,128]{1,0:T(8,128)} %param.15), kind=kLoop, calls=%fused_computation.19 | loop fusion | flops 2227200 | bytes 3674112 | tf_op jit(solution)/shard_map/reduce_max | solution.py:124
  141.7 0.1 select_reduce_fusion.1
  141.9 21.3 %pmax.7 = f32[64]{0:T(128)S(1)} all-reduce(f32[64]{0:T(128)S(1)} %select_reduce_fusion.1), channel_id=1, replica_groups=mesh['fsdp'=8,'rep'=4] {'fsdp'}, use_global_device_ids=true, to_apply=%region_4.5 | all-reduce | flops 64 | bytes 512 | tf_op jit(solution)/shard_map/pmax | solution.py:126
  163.2 0.1 select_reduce_fusion
  163.3 0.9 divide_convert_fusion
  164.3 0.1 reshape.145
  164.4 0.1 add_convert_fusion
  164.5 0.1 iota_compare_fusion.1
  164.6 0.3 fusion.50
  164.9 0.3 fusion.48
  165.3 44.7 %all-gather.2.cloned.1.call-done = bf16[8192,128]{1,0:T(8,128)(2,1)} async-done(((bf16[1024,128]{1,0:T(8,128)(2,1)}), bf16[8192,128]{1,0:T(8,128)(2,1)}) %all-gather.2.cloned.1.call-update) | async-done | bytes 2097168 | tf_op jit(solution)/shard_map/all_gather | solution.py:129
  210.0 2.2 fusion
  212.2 0.1 fusion.47
  212.3 0.1 fusion.37
  212.4 0.1 pad_maximum_fusion.1
  212.5 0.6 copy.32
  213.1 0.1 fusion.49
  213.2 0.1 fusion.51
  213.4 0.2 fusion.12
  213.5 0.2 fusion.14
  213.8 0.2 fusion.4
  214.0 0.2 fusion.11
  214.2 0.2 fusion.13
  214.5 0.2 fusion.3
  214.7 0.6 pad_maximum_fusion
  215.3 3.0 %copy.73 = bf16[8192,128]{1,0:T(8,128)(2,1)} copy(bf16[8192,128]{1,0:T(8,128)(2,1)} %all-gather.2.cloned.1.call-done) | data formatting | bytes 4194304
  (33 shorter events, 0.3 us)
Async XLA Ops:
  7.2 1.6 copy-start
  7.2 96.2 %reduce-scatter.2.cloned.1.call-start = ((), (), s32[]{:S(2)}) async-start(), calls=%async_computation.1 | async-start | bytes 4718592 | tf_op jit(solution)/shard_map/reduce_scatter | solution.py:109
  12.2 126.6 %all-reduce.2.cloned.1.call-start = ((), (), s32[]{:S(2)}) async-start(), calls=%async_computation.2 | async-start | bytes 1048576 | tf_op jit(solution)/shard_map/psum | solution.py:117
  103.4 106.5 %all-gather.2.cloned.1.call-start = ((), (), s32[]{:S(2)}) async-start(), calls=%async_computation.3 | async-start | bytes 2359296 | tf_op jit(solution)/shard_map/all_gather | solution.py:129
  103.5 60.8 %copy-start.4 = (bf16[2,2,8192]{2,1,0:T(2,128)(2,1)S(1)}, bf16[2,2,8192]{2,1,0:T(2,128)(2,1)}, u32[]{:S(2)}) copy-start(bf16[2,2,8192]{2,1,0:T(2,128)(2,1)} %param.16) | copy-start | bytes 196612
  103.5 60.9 %copy-start.6 = (s32[2]{0:T(128)S(1)}, s32[2]{0:T(128)}, u32[]{:S(2)}) copy-start(s32[2]{0:T(128)} %param.21) | copy-start | bytes 28
  103.5 61.0 %copy-start.5 = (bf16[2,2,1024]{2,1,0:T(2,128)(2,1)S(1)}, bf16[2,2,1024]{2,1,0:T(2,128)(2,1)}, u32[]{:S(2)}) copy-start(bf16[2,2,1024]{2,1,0:T(2,128)(2,1)} %param.17) | copy-start | bytes 24580
  103.5 61.0 %copy-start.1 = (bf16[2,1024,128]{2,1,0:T(8,128)(2,1)S(1)}, bf16[2,1024,128]{2,1,0:T(8,128)(2,1)}, u32[]{:S(2)}) copy-start(bf16[2,1024,128]{2,1,0:T(8,128)(2,1)} %param.19) | copy-start | bytes 1572868
  141.7 21.6 %copy-start.3 = (f32[1024,128]{1,0:T(8,128)}, f32[1024,128]{1,0:T(8,128)S(1)}, u32[]{:S(2)}) copy-start(f32[1024,128]{1,0:T(8,128)S(1)} %get-tuple-element.48) | copy-start | bytes 1572868
  164.3 49.3 %copy-start.2 = (bf16[2,1024,128]{2,1,0:T(8,128)(2,1)S(1)}, bf16[2,1024,128]{2,1,0:T(8,128)(2,1)}, u32[]{:S(2)}) copy-start(bf16[2,1024,128]{2,1,0:T(8,128)(2,1)} %param.20) | copy-start | bytes 1572868
  164.6 49.2 %copy-start.7 = (bf16[2,2,128]{2,1,0:T(2,128)(2,1)S(1)}, bf16[2,2,128]{2,1,0:T(2,128)(2,1)}, u32[]{:S(2)}) copy-start(bf16[2,2,128]{2,1,0:T(2,128)(2,1)} %param.18) | copy-start | bytes 3076
Sparse Core Ops, SparseCore 0:
  12.3 91.0 reduce-scatter.1
  105.8 33.0 all-reduce.1
  164.4 45.5 all-gather.1
where the time goes:
time: 225 us
  waiting for transfers between devices  171 us (76%)
  blocking collectives  21.3 us (9%)
  between operations  13.9 us (6%)
  matrix products  7.48 us (3%)
  other arithmetic  5.48 us (2%)
  local copies, waits for them, and re-layouts  5.36 us (2%)
    reduce_scatter x1, waiting for transfers between devices, shards(): lax.psum_scatter(lax.dot_general(tokens_x, cotangent, (((0,), (0,)), ((),...  91.1 us
    all_gather x1, waiting for transfers between devices, shards(): rollout_weight = lax.all_gather(local_quant, 'fsdp', axis=0, tiled=True)  44.7 us
    psum x1, waiting for transfers between devices, shards(): gradient = lax.psum(partial_grad, 'rep')  35.3 us
    pmax x1, blocking collectives, shards(): scales = lax.pmax(local_peaks, 'fsdp') + peak_eps  21.3 us
    unnamed x19, local copies, waits for them, and re-layouts  5.2 us
  transfers between devices with their start and end apart: 3, of which 3 were waited for; matrix products, arithmetic and copies ran while one was open for 0% of the time, Pallas kernels for 0%

commit v1 on v0

--- a/solution.py
+++ b/solution.py
@@ -1,8 +1,11 @@
+import functools
 import math
 
 import jax
 import jax.numpy as jnp
 from jax import lax
+from jax.experimental import pallas as pl
+from jax.experimental.pallas import tpu as pltpu
 from jax.sharding import PartitionSpec as P
 
 D = 8192
@@ -132,9 +135,396 @@
     return (weight_next, first_next, second_next, rollout_weight, fresh_keys, attended)
 
 
+MESH = pl.DeviceIdType.MESH
+F32 = jnp.float32
+BF16 = jnp.bfloat16
+TAIL = 16
+
+
+def tdot(a, b):
+    return lax.dot_general(a, b, (((0,), (0,)), ((), ())), preferred_element_type=F32)
+
+
+def step_kernel(
+    nz, tok, cot, wt, mo, ve, hid, qr, nv, kc, vc, lens, cosr, sinr,
+    w_o, m_o, v_o, roll_o, fk_o, att_o,
+    sib, sibcot, rs_s, rs_r, keep_b, keep_own, z_s, z_r, g_q, ag, qs, ex, mx, sm,
+    sib_ss, sib_rs, rs_ss, rs_rs, z_ss, z_rs, g_ss, g_rs,
+    az_ss, az_rs, ap_ss, ap_rs, as_ss, as_rs, o_s,
+):
+    f = lax.axis_index("fsdp")
+    r = lax.axis_index("rep")
+    z, x = lax.div(f, 2), lax.rem(f, 2)
+    y, c = lax.div(r, 2), lax.rem(r, 2)
+    shard = wt.shape[0]
+    half = shard // 2
+    quarter = shard // 4
+    blocks = quarter // BLOCK
+    steps, rows, joined = qr.shape
+    hd = kc.shape[2]
+    heads = joined // hd
+
+    def flip(value, bit):
+        return 1 - value if bit else value
+
+    def device(dz=0, dx=0, dy=0, dc=0):
+        zz = lax.rem(z + dz, nz) if dz else z
+        return {"fsdp": zz * 2 + flip(x, dx), "rep": flip(y, dy) * 2 + flip(c, dc)}
+
+    def remote(src, dst, ss, rs, where):
+        return pltpu.make_async_remote_copy(
+            src_ref=src, dst_ref=dst, send_sem=ss, recv_sem=rs,
+            device_id=where, device_id_type=MESH,
+        )
+
+    sibling = device(dc=1)
+    xn, yn = device(dx=1), device(dy=1)
+    zpeer = [device(dz=1 + j) for j in range(nz - 1)]
+    barrier = pltpu.get_barrier_semaphore()
+    peers = [sibling, xn, yn] + zpeer
+    for peer in peers:
+        pl.semaphore_signal(barrier, inc=1, device_id=peer, device_id_type=MESH)
+
+    scale = 1.0 / math.sqrt(hd)
+    for i in range(rows):
+        for s in range(steps):
+            for h in range(heads):
+                qs[i, s * heads + h : s * heads + h + 1, :] = qr[
+                    s, i : i + 1, h * hd : (h + 1) * hd
+                ].astype(F32)
+    for i in range(rows):
+        sc = lax.dot_general(
+            qs[i].astype(BF16), kc[i], (((1,), (1,)), ((), ())), preferred_element_type=F32
+        ) * scale
+        slot = lax.broadcasted_iota(jnp.int32, sc.shape, 1)
+        sc = jnp.where(slot < lens[i], sc, -jnp.inf)
+        top = jnp.max(sc, axis=1, keepdims=True)
+        e = jnp.exp(sc - top)
+        ex[i] = e
+        mx[i] = jnp.broadcast_to(top, mx.shape[1:])
+        sm[i] = jnp.broadcast_to(jnp.sum(e, axis=1, keepdims=True), sm.shape[1:])
+
+    pl.semaphore_wait(barrier, len(peers))
+
+    def target(j):
+        return lax.rem(z + 1 + j, nz)
+
+    sends = []
+
+    def go(copy):
+        copy.start()
+        sends.append(copy)
+        return copy
+
+    cot_in = go(remote(cot, sibcot, sib_ss.at[2 * nz], sib_rs.at[2 * nz], sibling))
+    sib_in = {}
+    for j in range(nz):
+        for dx in (1, 0):
+            k = 2 * j + dx
+            off = pl.multiple_of((target(j) * 2 + flip(x, dx)) * shard + (1 - c) * half, BLOCK)
+            sib_in[j, dx] = go(
+                remote(tok.at[:, pl.ds(off, half)], sib.at[k], sib_ss.at[k], sib_rs.at[k], sibling)
+            )
+    cot_in.wait_recv()
+
+    def part(j, dx, dy):
+        at = flip(y, dy) * quarter
+        off = pl.multiple_of((target(j) * 2 + flip(x, dx)) * shard + c * half + at, BLOCK)
+        at = pl.multiple_of(at, BLOCK)
+        return tdot(tok[:, pl.ds(off, quarter)], cot[...]) + tdot(
+            sib[2 * j + dx, :, pl.ds(at, quarter)], sibcot[...]
+        )
+
+    def first(j):
+        return (1, 0) if j % 2 == 0 else (0, 1)
+
+    rs_in = {}
+
+    def stage_a(j):
+        da = first(j)
+        near, far = (xn, yn) if j % 2 == 0 else (yn, xn)
+        sib_in[j, 1].wait_recv()
+        if j % 2:
+            sib_in[j, 0].wait_recv()
+        rs_s[1, j] = part(j, 1, 1).astype(BF16)
+        rs_in[1, j] = go(remote(rs_s.at[1, j], rs_r.at[1, j], rs_ss.at[1, j], rs_rs.at[1, j], near))
+        rs_s[0, j] = part(j, *da).astype(BF16)
+        rs_in[0, j] = go(remote(rs_s.at[0, j], rs_r.at[0, j], rs_ss.at[0, j], rs_rs.at[0, j], near))
+        if j % 2 == 0:
+            sib_in[j, 0].wait_recv()
+        keep_b[j] = part(j, da[1], da[0])
+        keep_own[j] = part(j, 0, 0)
+
+    def stage_b(j):
+        far = yn if j % 2 == 0 else xn
+        rs_in[1, j].wait_recv()
+        rs_s[2, j] = (keep_b[j] + rs_r[1, j].astype(F32)).astype(BF16)
+        rs_in[2, j] = go(remote(rs_s.at[2, j], rs_r.at[2, j], rs_ss.at[2, j], rs_rs.at[2, j], far))
+
+    z_in = {}
+
+    def stage_z(j):
+        rs_in[0, j].wait_recv()
+        rs_in[2, j].wait_recv()
+        total = keep_own[j] + rs_r[0, j].astype(F32) + rs_r[2, j].astype(F32)
+        if j == nz - 1:
+            return total
+        z_s[j] = total.astype(BF16)
+        z_in[j] = go(remote(z_s.at[j], z_r.at[j], z_ss.at[j], z_rs.at[j], zpeer[j]))
+        return None
+
+    for j in range(nz):
+        stage_a(j)
+    stage_b(0)
+    for j in range(1, nz):
+        stage_b(j)
+        stage_z(j - 1)
+    grad = stage_z(nz - 1)
+    for j in range(nz - 1):
+        z_in[j].wait_recv()
+        grad = grad + z_r[j].astype(F32)
+    g_q[0] = grad
+    g_in = {
+        2: go(remote(g_q.at[0], g_q.at[2], g_ss.at[2], g_rs.at[2], sibling)),
+    }
+
+    def update(gradient, dy, dc):
+        at = pl.ds(pl.multiple_of((flip(c, dc) * 2 + flip(y, dy)) * quarter, BLOCK), quarter)
+        new = adamw(wt[at, :], mo[at, :], ve[at, :], gradient)
+        w_o[at, :], m_o[at, :], v_o[at, :] = new
+        return new[0]
+
+    fresh = update(grad, 0, 0)
+    row = lax.broadcasted_iota(jnp.int32, (TAIL, hd), 0)
+    tail = jnp.zeros((TAIL, hd), F32)
+    for b in range(blocks):
+        piece = fresh[b * BLOCK : (b + 1) * BLOCK]
+        peak = jnp.max(jnp.max(jnp.abs(piece), axis=0, keepdims=True), axis=1, keepdims=True)
+        peak = peak + peak_eps
+        ag[0, 0, nz - 1, b * BLOCK : (b + 1) * BLOCK] = (piece / peak).astype(BF16)
+        rest = jnp.broadcast_to(peak, (TAIL, hd))
+        for k in range(3):
+            high = rest.astype(BF16).astype(F32)
+            tail = jnp.where(row == 3 * b + k, high, tail)
+            rest = rest - high
+    ag[0, 0, nz - 1, quarter : quarter + TAIL] = tail.astype(BF16)
+
+    az_in = {
+        j: go(remote(ag.at[0, 0, nz - 1], ag.at[0, 0, j], az_ss.at[j], az_rs.at[j], zpeer[j]))
+        for j in range(nz - 1)
+    }
+    outs = []
+    raw = [jnp.zeros((steps * rows, hd), F32)]
+    ap_in, as_in = {}, {}
+
+    def place(dc, p, j):
+        shard_at = lax.rem(z + nz - 1 - j, nz) * 2 + flip(x, p & 1)
+        return shard_at * shard + (flip(c, dc) * 2 + flip(y, p >> 1)) * quarter
+
+    def emit(dc, p, j):
+        n = (dc * 4 + p) * nz + j
+        copy = pltpu.make_async_copy(
+            ag.at[dc, p, j, pl.ds(0, quarter)],
+            roll_o.at[pl.ds(pl.multiple_of(place(dc, p, j), BLOCK), quarter)],
+            o_s.at[n],
+        )
+        copy.start()
+        outs.append(copy)
+
+    def project(dc, p, j):
+        at = place(dc, p, j)
+        t = ag[dc, p, j, quarter : quarter + TAIL].astype(F32)
+        for b in range(blocks):
+            peak = t[3 * b : 3 * b + 1] + t[3 * b + 1 : 3 * b + 2] + t[3 * b + 2 : 3 * b + 3]
+            h = hid[:, pl.ds(pl.multiple_of(at + b * BLOCK, BLOCK), BLOCK)]
+            got = jnp.dot(
+                h, ag[dc, p, j, b * BLOCK : (b + 1) * BLOCK], preferred_element_type=F32
+            )
+            raw[0] = raw[0] + got * peak
+
+    def share(p, j):
+        as_in[p, j] = go(
+            remote(ag.at[0, p, j], ag.at[1, p, j], as_ss.at[p, j], as_rs.at[p, j], sibling)
+        )
+
+    def plane(src, p, j, where):
+        ap_in[p, j] = go(
+            remote(ag.at[0, src, j], ag.at[0, p, j], ap_ss.at[p - 1, j], ap_rs.at[p - 1, j], where)
+        )
+
+    def spread(j):
+        if j < nz - 1:
+            az_in[j].wait_recv()
+        plane(0, 1, j, xn)
+        plane(0, 2, j, yn)
+        share(0, j)
+        emit(0, 0, j)
+        project(0, 0, j)
+
+    def relay(j):
+        ap_in[1, j].wait_recv()
+        if j % 2 == 0:
+            plane(1, 3, j, yn)
+        share(1, j)
+        ap_in[2, j].wait_recv()
+        if j % 2 == 1:
+            plane(2, 3, j, xn)
+        share(2, j)
+        emit(0, 1, j)
+        emit(0, 2, j)
+        project(0, 1, j)
+        project(0, 2, j)
+
+    def last(j):
+        ap_in[3, j].wait_recv()
+        share(3, j)
+        emit(0, 3, j)
+        project(0, 3, j)
+
+    def cross(p, j):
+        as_in[p, j].wait_recv()
+        emit(1, p, j)
+        project(1, p, j)
+
+    spread(nz - 1)
+    g_in[1] = go(remote(g_q.at[0], g_q.at[1], g_ss.at[1], g_rs.at[1], yn))
+    g_in[2].wait_recv()
+    update(g_q[2], 0, 1)
+    order = [nz - 1] + list(range(nz - 1))
+    for i in range(1, nz):
+        spread(order[i])
+        relay(order[i - 1])
+        cross(0, order[i - 1])
+    g_in[1].wait_recv()
+    g_in[3] = go(remote(g_q.at[1], g_q.at[3], g_ss.at[3], g_rs.at[3], sibling))
+    update(g_q[1], 1, 0)
+    relay(order[-1])
+    g_in[3].wait_recv()
+    update(g_q[3], 1, 1)
+    for j in order:
+        last(j)
+    cross(0, order[-1])
+    for p in (1, 2, 3):
+        for j in order:
+            cross(p, j)
+
+    keys = raw[0] * cosr[...] + pltpu.roll(raw[0], hd // 2, 1) * sinr[...]
+    keys = keys.astype(BF16)
+    for s in range(steps):
+        fk_o[s] = keys[s * rows : (s + 1) * rows]
+    keys = keys.astype(F32)
+    step_of = lax.broadcasted_iota(jnp.int32, (steps * heads, 1), 0) // heads
+    lines = [[] for _ in range(steps)]
+    for i in range(rows):
+        query = qs[i]
+        top_c = mx[i][:, :1]
+        sum_c = sm[i][:, :1]
+        top = top_c
+        scf = []
+        for t in range(steps):
+            k = keys[t * rows + i : t * rows + i + 1]
+            sc = jnp.sum(query * k, axis=1, keepdims=True) * scale
+            sc = jnp.where(step_of >= t, sc, -jnp.inf)
+            scf.append(sc)
+            top = jnp.maximum(top, sc)
+        exf = [jnp.exp(sc - top) for sc in scf]
+        fix = jnp.exp(top_c - top)
+        total = sum_c * fix
+        for e in exf:
+            total = total + e
+        prob = (ex[i] * (fix / total)).astype(BF16)
+        mixed = jnp.dot(prob, vc[i], preferred_element_type=F32)
+        for t in range(steps):
+            pf = (exf[t] / total).astype(BF16).astype(F32)
+            mixed = mixed + pf * nv[t, i : i + 1, :].astype(F32)
+        for s in range(steps):
+            lines[s].append(
+                jnp.concatenate(
+                    [mixed[s * heads + h : s * heads + h + 1] for h in range(heads)], axis=1
+                )
+            )
+    for s in range(steps):
+        att_o[s] = jnp.concatenate(lines[s], axis=0).astype(BF16)
+    for copy in sends:
+        copy.wait_send()
+    for copy in outs:
+        copy.wait()
+
+
+def fused(
+    nz, tokens_x, cotangent, master_weight, first_moment, second_moment,
+    hidden_dec, queries, new_values, key_cache, value_cache, cache_lengths,
+):
+    steps, rows, width = hidden_dec.shape
+    shard, hd = master_weight.shape
+    quarter = shard // 4
+    slots = key_cache.shape[1]
+    qrows = queries.shape[2] // hd * steps
+    tokens = tokens_x.shape[0]
+    half = hd // 2
+    freq = rope_theta ** (-jnp.arange(half, dtype=F32) * 2.0 / hd)
+    positions = cache_lengths[None, :] + jnp.arange(steps, dtype=jnp.int32)[:, None]
+    angle = positions.astype(F32).reshape(-1, 1) * freq
+    cosine, sine = jnp.cos(angle), jnp.sin(angle)
+    cosr = jnp.concatenate([cosine, cosine], axis=1)
+    sinr = jnp.concatenate([-sine, sine], axis=1)
+    vm = pl.BlockSpec(memory_space=pltpu.VMEM)
+    dma = pltpu.SemaphoreType.DMA
+    shape = jax.ShapeDtypeStruct
+    return pl.pallas_call(
+        functools.partial(step_kernel, nz),
+        out_shape=(
+            shape((shard, hd), F32), shape((shard, hd), F32), shape((shard, hd), F32),
+            shape((width, hd), BF16), shape(new_values.shape, BF16), shape(queries.shape, BF16),
+        ),
+        in_specs=[vm] * 10 + [pl.BlockSpec(memory_space=pltpu.SMEM)] + [vm] * 2,
+        out_specs=(vm, vm, vm, pl.BlockSpec(memory_space=pl.ANY), vm, vm),
+        scratch_shapes=[
+            pltpu.VMEM((2 * nz, tokens, shard // 2), BF16),
+            pltpu.VMEM((tokens, hd), BF16),
+            pltpu.VMEM((3, nz, quarter, hd), BF16),
+            pltpu.VMEM((3, nz, quarter, hd), BF16),
+            pltpu.VMEM((nz, quarter, hd), F32),
+            pltpu.VMEM((nz, quarter, hd), F32),
+            pltpu.VMEM((nz - 1, quarter, hd), BF16),
+            pltpu.VMEM((nz - 1, quarter, hd), BF16),
+            pltpu.VMEM((4, quarter, hd), F32),
+            pltpu.VMEM((2, 4, nz, quarter + TAIL, hd), BF16),
+            pltpu.VMEM((rows, qrows, hd), F32),
+            pltpu.VMEM((rows, qrows, slots), F32),
+            pltpu.VMEM((rows, qrows, hd), F32),
+            pltpu.VMEM((rows, qrows, hd), F32),
+            dma((2 * nz + 1,)), dma((2 * nz + 1,)),
+            dma((3, nz)), dma((3, nz)),
+            dma((nz - 1,)), dma((nz - 1,)),
+            dma((4,)), dma((4,)),
+            dma((nz - 1,)), dma((nz - 1,)),
+            dma((3, nz)), dma((3, nz)),
+            dma((4, nz)), dma((4, nz)),
+            dma((8 * nz,)),
+        ],
+        compiler_params=pltpu.CompilerParams(
+            collective_id=0, has_side_effects=True, vmem_limit_bytes=40 * 1024 * 1024
+        ),
+        name="step",
+    )(
+        tokens_x, cotangent, master_weight, first_moment, second_moment,
+        hidden_dec.reshape(steps * rows, width), queries, new_values,
+        key_cache, value_cache, cache_lengths, cosr, sinr,
+    )
+
+
+def body(parts, replicas, *args):
+    quarter, left = divmod(args[2].shape[0], 4)
+    fits = replicas == 4 and parts >= 4 and parts % 2 == 0 and left == 0 and quarter % BLOCK == 0
+    if fits and quarter // BLOCK * 3 <= TAIL:
+        return fused(parts // 2, *args)
+    return shards(*args)
+
+
 def solution(mesh):
     return jax.shard_map(
-        shards,
+        functools.partial(body, mesh.shape["fsdp"], mesh.shape["rep"]),
         mesh=mesh,
         in_specs=(
             P(("fsdp", "rep"), None),

time: 225 us -> 62.5 us (0.28)
  waiting for transfers between devices: 171 us -> 0 us
  Pallas kernels: 0 us -> 45 us
  blocking collectives: 21.3 us -> 0 us
  between operations: 13.9 us -> 0.67 us
  local copies, waits for them, and re-layouts: 5.36 us -> 15.4 us
  matrix products: 7.48 us -> 0 us
  other arithmetic: 5.48 us -> 0.86 us
    reduce_scatter x1 -> x0, waiting for transfers between devices: 91.1 us -> none  [shards(): lax.psum_scatter(lax.dot_general(tokens_x, cotangent, (((0,), (0,)), ((),...]
    pallas_call x0 -> x1, Pallas kernels: none -> 45 us  [fused(): pl.pallas_call(functools.partial(step_kernel, nz), out_shape=(shape((shar...]
    all_gather x1 -> x0, waiting for transfers between devices: 44.7 us -> none  [shards(): rollout_weight = lax.all_gather(local_quant, 'fsdp', axis=0, tiled=True)]
    psum x1 -> x0, waiting for transfers between devices: 35.3 us -> none  [shards(): gradient = lax.psum(partial_grad, 'rep')]
    pmax x1 -> x0, blocking collectives: 21.3 us -> none  [shards(): scales = lax.pmax(local_peaks, 'fsdp') + peak_eps]
    unnamed x19 -> x26, local copies, waits for them, and re-layouts: 5.2 us -> 14.4 us
    dot_general x10 -> x0, matrix products: 7.48 us -> none  [the longest x1 3.43 us: shards(): lax.dot_general(tokens_x, cotangent, (((0,), (0,)), ((), ())), preferred_...]
    reduce_max x2 -> x0, other arithmetic: 3.02 us -> none  [the longest x1 2.9 us: shards(): row_peak = jnp.max(jnp.abs(weight_next), axis=1)]
  transfers between devices with their start and end apart: 3 -> 0, of which waited for: 3 -> 0; matrix products, arithmetic and copies ran while one was open for 0% -> 0% of each run, Pallas kernels for 0% -> 0%
where the time goes in v1:
time: 62.5 us; the launch traced here: 61.9 us
  Pallas kernels  45 us (72%)
  local copies, waits for them, and re-layouts  15.4 us (25%)
  other arithmetic  0.86 us (1%)
  between operations  0.67 us (1%)
    pallas_call x1, Pallas kernels, fused(): pl.pallas_call(functools.partial(step_kernel, nz), out_shape=(shape((shar...  45 us
    unnamed x26, local copies, waits for them, and re-layouts  14.4 us

profile of v1, /device:TPU:0, one launch (start us, length us, event | category | flops | bytes accessed | tf_op | source)
XLA Modules:
  0.0 61.9 jit_solution(16761818189967429358)
XLA Ops:
  0.6 0.7 %add_convert_fusion = f32[2,2]{1,0:T(2,128)S(1)} fusion(s32[2]{0:T(128)} %lens.1), kind=kLoop, calls=%fused_computation.4 | loop fusion | flops 8 | bytes 24 | tf_op jit(solution)/shard_map/convert_element_type | solution.py:467
  1.3 0.1 convert_element_type.11
  1.4 0.1 fusion
  1.5 0.1 pad_maximum_fusion
  1.6 0.9 %reshape.39.hid = bf16[4,8192]{1,0:T(4,128)(2,1)S(1)} reshape(bf16[2,2,8192]{2,1,0:T(2,128)(2,1)} %param.16) | data formatting | bytes 131072 | tf_op jit(solution)/shard_map/reshape | solution.py:512
  2.5 0.0 copy-start
  2.5 1.6 %copy-done = bf16[128,8192]{1,0:T(8,128)(2,1)S(1)} copy-done((bf16[128,8192]{1,0:T(8,128)(2,1)S(1)}, bf16[128,8192]{1,0:T(8,128)(2,1)}, u32[]{:S(2)}) %copy-start) | copy-done | bytes 2097176
  4.1 0.0 copy-start.1
  4.1 1.0 %copy-done.1 = f32[1024,128]{1,0:T(8,128)S(1)} copy-done((f32[1024,128]{1,0:T(8,128)S(1)}, f32[1024,128]{1,0:T(8,128)}, u32[]{:S(2)}) %copy-start.1) | copy-done | bytes 524312
  5.1 0.0 copy-start.2
  5.1 1.0 %copy-done.2 = f32[1024,128]{1,0:T(8,128)S(1)} copy-done((f32[1024,128]{1,0:T(8,128)S(1)}, f32[1024,128]{1,0:T(8,128)}, u32[]{:S(2)}) %copy-start.2) | copy-done | bytes 524312
  6.1 0.0 copy-start.3
  6.1 1.0 %copy-done.3 = f32[1024,128]{1,0:T(8,128)S(1)} copy-done((f32[1024,128]{1,0:T(8,128)S(1)}, f32[1024,128]{1,0:T(8,128)}, u32[]{:S(2)}) %copy-start.3) | copy-done | bytes 524312
  7.2 0.0 copy-start.4
  7.2 1.0 %copy-done.4 = bf16[2,1024,128]{2,1,0:T(8,128)(2,1)S(1)} copy-done((bf16[2,1024,128]{2,1,0:T(8,128)(2,1)S(1)}, bf16[2,1024,128]{2,1,0:T(8,128)(2,1)}, u32[]{:S(2)}) %copy-start.4) | copy-done | bytes 524312
  8.2 0.0 copy-start.5
  8.2 1.0 %copy-done.5 = bf16[2,1024,128]{2,1,0:T(8,128)(2,1)S(1)} copy-done((bf16[2,1024,128]{2,1,0:T(8,128)(2,1)S(1)}, bf16[2,1024,128]{2,1,0:T(8,128)(2,1)}, u32[]{:S(2)}) %copy-start.5) | copy-done | bytes 524312
  9.3 0.0 copy-start.6
  9.3 0.8 %copy-done.6 = bf16[128,128]{1,0:T(8,128)(2,1)S(1)} copy-done((bf16[128,128]{1,0:T(8,128)(2,1)S(1)}, bf16[128,128]{1,0:T(8,128)(2,1)}, u32[]{:S(2)}) %copy-start.6) | copy-done | bytes 32792
  10.0 0.0 copy-start.7
  10.0 0.7 %copy-done.7 = bf16[2,2,1024]{2,1,0:T(2,128)(2,1)S(1)} copy-done((bf16[2,2,1024]{2,1,0:T(2,128)(2,1)S(1)}, bf16[2,2,1024]{2,1,0:T(2,128)(2,1)}, u32[]{:S(2)}) %copy-start.7) | copy-done | bytes 8216
  10.7 0.0 copy-start.8
  10.7 0.7 %copy-done.8 = bf16[2,2,128]{2,1,0:T(2,128)(2,1)S(1)} copy-done((bf16[2,2,128]{2,1,0:T(2,128)(2,1)S(1)}, bf16[2,2,128]{2,1,0:T(2,128)(2,1)}, u32[]{:S(2)}) %copy-start.8) | copy-done | bytes 1048
  11.4 0.0 copy-start.9
  11.4 0.7 %copy-done.9 = s32[2]{0:T(128)S(1)} copy-done((s32[2]{0:T(128)S(1)}, s32[2]{0:T(128)}, u32[]{:S(2)}) %copy-start.9) | copy-done | bytes 32
  12.1 45.0 %step.1 = (f32[1024,128]{1,0:T(8,128)S(1)}, f32[1024,128]{1,0:T(8,128)S(1)}, f32[1024,128]{1,0:T(8,128)S(1)}, bf16[8192,128]{1,0:T(8,128)(2,1)S(1)}, bf16[2,2,12...) custom-call(bf16[128,8192]{1,0:T(8,128)(2,1)S(1)} %copy-done, bf16[128,128]{1,0:T(8,128)(2,1)S(1)} %copy-done.6, ...), custom_call_target="tpu_custom_call" | custom-call | tf_op jit(solution)/shard_map/step/pallas_call | solution.py:474
  57.0 0.8 %copy.23 = f32[1024,128]{1,0:T(8,128)} copy(f32[1024,128]{1,0:T(8,128)S(1)} %get-tuple-element.17) | data formatting | bytes 1048576
  57.8 0.8 %copy.24 = f32[1024,128]{1,0:T(8,128)} copy(f32[1024,128]{1,0:T(8,128)S(1)} %get-tuple-element.18) | data formatting | bytes 1048576
  58.6 0.8 %copy.25 = f32[1024,128]{1,0:T(8,128)} copy(f32[1024,128]{1,0:T(8,128)S(1)} %get-tuple-element.19) | data formatting | bytes 1048576
  59.4 1.3 %copy.26 = bf16[8192,128]{1,0:T(8,128)(2,1)} copy(bf16[8192,128]{1,0:T(8,128)(2,1)S(1)} %get-tuple-element.20) | data formatting | bytes 4194304
  60.8 0.6 copy.27
  61.3 0.6 copy.28
  (1 shorter events, 0.0 us)
Async XLA Ops:
  2.5 1.6 %copy-start = (bf16[128,8192]{1,0:T(8,128)(2,1)S(1)}, bf16[128,8192]{1,0:T(8,128)(2,1)}, u32[]{:S(2)}) copy-start(bf16[128,8192]{1,0:T(8,128)(2,1)} %tok.1) | copy-start | bytes 6291460
  4.1 1.0 %copy-start.1 = (f32[1024,128]{1,0:T(8,128)S(1)}, f32[1024,128]{1,0:T(8,128)}, u32[]{:S(2)}) copy-start(f32[1024,128]{1,0:T(8,128)} %wt.1) | copy-start | bytes 1572868
  5.1 1.0 %copy-start.2 = (f32[1024,128]{1,0:T(8,128)S(1)}, f32[1024,128]{1,0:T(8,128)}, u32[]{:S(2)}) copy-start(f32[1024,128]{1,0:T(8,128)} %mo.1) | copy-start | bytes 1572868
  6.1 1.0 %copy-start.3 = (f32[1024,128]{1,0:T(8,128)S(1)}, f32[1024,128]{1,0:T(8,128)}, u32[]{:S(2)}) copy-start(f32[1024,128]{1,0:T(8,128)} %ve.1) | copy-start | bytes 1572868
  7.2 1.0 %copy-start.4 = (bf16[2,1024,128]{2,1,0:T(8,128)(2,1)S(1)}, bf16[2,1024,128]{2,1,0:T(8,128)(2,1)}, u32[]{:S(2)}) copy-start(bf16[2,1024,128]{2,1,0:T(8,128)(2,1)} %kc.1) | copy-start | bytes 1572868
  8.2 1.0 %copy-start.5 = (bf16[2,1024,128]{2,1,0:T(8,128)(2,1)S(1)}, bf16[2,1024,128]{2,1,0:T(8,128)(2,1)}, u32[]{:S(2)}) copy-start(bf16[2,1024,128]{2,1,0:T(8,128)(2,1)} %vc.1) | copy-start | bytes 1572868
  9.3 0.8 %copy-start.6 = (bf16[128,128]{1,0:T(8,128)(2,1)S(1)}, bf16[128,128]{1,0:T(8,128)(2,1)}, u32[]{:S(2)}) copy-start(bf16[128,128]{1,0:T(8,128)(2,1)} %cot.1) | copy-start | bytes 98308
  10.0 0.7 %copy-start.7 = (bf16[2,2,1024]{2,1,0:T(2,128)(2,1)S(1)}, bf16[2,2,1024]{2,1,0:T(2,128)(2,1)}, u32[]{:S(2)}) copy-start(bf16[2,2,1024]{2,1,0:T(2,128)(2,1)} %qr.1) | copy-start | bytes 24580
  10.7 0.7 %copy-start.8 = (bf16[2,2,128]{2,1,0:T(2,128)(2,1)S(1)}, bf16[2,2,128]{2,1,0:T(2,128)(2,1)}, u32[]{:S(2)}) copy-start(bf16[2,2,128]{2,1,0:T(2,128)(2,1)} %nv.1) | copy-start | bytes 3076
  11.4 0.7 %copy-start.9 = (s32[2]{0:T(128)S(1)}, s32[2]{0:T(128)}, u32[]{:S(2)}) copy-start(s32[2]{0:T(128)} %lens.1) | copy-start | bytes 28

commit v2 on v1

--- a/solution.py
+++ b/solution.py
@@ -146,11 +146,12 @@
 
 
 def step_kernel(
-    nz, tok, cot, wt, mo, ve, hid, qr, nv, kc, vc, lens, cosr, sinr,
-    w_o, m_o, v_o, roll_o, fk_o, att_o,
-    sib, sibcot, rs_s, rs_r, keep_b, keep_own, z_s, z_r, g_q, ag, qs, ex, mx, sm,
+    nz, tok_h, cot_h, wt_h, mo_h, ve_h, hid_h, qr_h, nv_h, kc_h, vc_h, lens_h,
+    w_o, m_o, v_o, ag, raw_o, qs, ex, mx, sm, vc, nv,
+    tok, cot, wt, mo, ve, hid3, hid, qr, kc, lens, in_s,
+    sib, sibcot, rs_s, rs_r, keep_b, keep_own, z_s, z_r, g_q,
     sib_ss, sib_rs, rs_ss, rs_rs, z_ss, z_rs, g_ss, g_rs,
-    az_ss, az_rs, ap_ss, ap_rs, as_ss, as_rs, o_s,
+    az_ss, az_rs, ap_ss, ap_rs, as_ss, as_rs,
 ):
     f = lax.axis_index("fsdp")
     r = lax.axis_index("rep")
@@ -184,6 +185,19 @@
     peers = [sibling, xn, yn] + zpeer
     for peer in peers:
         pl.semaphore_signal(barrier, inc=1, device_id=peer, device_id_type=MESH)
+
+    loads = [
+        pltpu.make_async_copy(a, b, in_s.at[n])
+        for n, (a, b) in enumerate((
+            (tok_h, tok), (cot_h, cot), (qr_h, qr), (kc_h, kc), (lens_h, lens), (hid_h, hid3),
+            (wt_h, wt), (mo_h, mo), (ve_h, ve), (vc_h, vc), (nv_h, nv),
+        ))
+    ]
+    for load in loads:
+        load.start()
+    for load in loads[2:6]:
+        load.wait()
+    hid[...] = jnp.concatenate([hid3[s].astype(F32) for s in range(steps)], axis=0).astype(BF16)
 
     scale = 1.0 / math.sqrt(hd)
     for i in range(rows):
@@ -204,6 +218,17 @@
         mx[i] = jnp.broadcast_to(top, mx.shape[1:])
         sm[i] = jnp.broadcast_to(jnp.sum(e, axis=1, keepdims=True), sm.shape[1:])
 
+    row = lax.broadcasted_iota(jnp.int32, (steps * rows, hd), 0)
+    lane = lax.broadcasted_iota(jnp.int32, (steps * rows, hd), 1)
+    position = row // rows
+    for i in range(rows):
+        position = position + jnp.where(row % rows == i, lens[i], 0)
+    freq = jnp.exp((lane % (hd // 2)).astype(F32) * (-2.0 * math.log(rope_theta) / hd))
+    angle = position.astype(F32) * freq
+    cosr = jnp.cos(angle)
+    sine = jnp.sin(angle)
+    sinr = jnp.where(lane < hd // 2, -sine, sine)
+
     pl.semaphore_wait(barrier, len(peers))
 
     def target(j):
@@ -216,16 +241,18 @@
         sends.append(copy)
         return copy
 
-    cot_in = go(remote(cot, sibcot, sib_ss.at[2 * nz], sib_rs.at[2 * nz], sibling))
+    cot_in = go(remote(cot_h, sibcot, sib_ss.at[2 * nz], sib_rs.at[2 * nz], sibling))
     sib_in = {}
     for j in range(nz):
         for dx in (1, 0):
             k = 2 * j + dx
             off = pl.multiple_of((target(j) * 2 + flip(x, dx)) * shard + (1 - c) * half, BLOCK)
             sib_in[j, dx] = go(
-                remote(tok.at[:, pl.ds(off, half)], sib.at[k], sib_ss.at[k], sib_rs.at[k], sibling)
+                remote(tok_h.at[:, pl.ds(off, half)], sib.at[k], sib_ss.at[k], sib_rs.at[k], sibling)
             )
     cot_in.wait_recv()
+    loads[0].wait()
+    loads[1].wait()
 
     def part(j, dx, dy):
         at = flip(y, dy) * quarter
@@ -294,6 +321,8 @@
         w_o[at, :], m_o[at, :], v_o[at, :] = new
         return new[0]
 
+    for load in loads[6:]:
+        load.wait()
     fresh = update(grad, 0, 0)
     row = lax.broadcasted_iota(jnp.int32, (TAIL, hd), 0)
     tail = jnp.zeros((TAIL, hd), F32)
@@ -313,23 +342,12 @@
         j: go(remote(ag.at[0, 0, nz - 1], ag.at[0, 0, j], az_ss.at[j], az_rs.at[j], zpeer[j]))
         for j in range(nz - 1)
     }
-    outs = []
     raw = [jnp.zeros((steps * rows, hd), F32)]
     ap_in, as_in = {}, {}
 
     def place(dc, p, j):
         shard_at = lax.rem(z + nz - 1 - j, nz) * 2 + flip(x, p & 1)
         return shard_at * shard + (flip(c, dc) * 2 + flip(y, p >> 1)) * quarter
-
-    def emit(dc, p, j):
-        n = (dc * 4 + p) * nz + j
-        copy = pltpu.make_async_copy(
-            ag.at[dc, p, j, pl.ds(0, quarter)],
-            roll_o.at[pl.ds(pl.multiple_of(place(dc, p, j), BLOCK), quarter)],
-            o_s.at[n],
-        )
-        copy.start()
-        outs.append(copy)
 
     def project(dc, p, j):
         at = place(dc, p, j)
@@ -358,32 +376,27 @@
         plane(0, 1, j, xn)
         plane(0, 2, j, yn)
         share(0, j)
-        emit(0, 0, j)
         project(0, 0, j)
 
     def relay(j):
         ap_in[1, j].wait_recv()
-        if j % 2 == 0:
+        if j == 0:
             plane(1, 3, j, yn)
         share(1, j)
         ap_in[2, j].wait_recv()
-        if j % 2 == 1:
+        if j != 0:
             plane(2, 3, j, xn)
         share(2, j)
-        emit(0, 1, j)
-        emit(0, 2, j)
         project(0, 1, j)
         project(0, 2, j)
 
     def last(j):
         ap_in[3, j].wait_recv()
         share(3, j)
-        emit(0, 3, j)
         project(0, 3, j)
 
     def cross(p, j):
         as_in[p, j].wait_recv()
-        emit(1, p, j)
         project(1, p, j)
 
     spread(nz - 1)
@@ -408,7 +421,47 @@
         for j in order:
             cross(p, j)
 
-    keys = raw[0] * cosr[...] + pltpu.roll(raw[0], hd // 2, 1) * sinr[...]
+    raw_o[...] = raw[0] * cosr + pltpu.roll(raw[0], hd // 2, 1) * sinr
+    for copy in sends:
+        copy.wait_send()
+
+
+def finish_kernel(
+    nz, w, m, v, ag, keys_ref, qs, ex, mx, sm, vc, nv,
+    w_h, m_h, v_h, roll_h, fk_h, att_h, fk_o, att_o, o_s, t_s,
+):
+    f = lax.axis_index("fsdp")
+    r = lax.axis_index("rep")
+    z, x = lax.div(f, 2), lax.rem(f, 2)
+    y, c = lax.div(r, 2), lax.rem(r, 2)
+    shard, hd = w.shape
+    quarter = shard // 4
+    rows = qs.shape[0]
+    steps = keys_ref.shape[0] // rows
+    heads = qs.shape[1] // steps
+    scale = 1.0 / math.sqrt(hd)
+
+    def flip(value, bit):
+        return 1 - value if bit else value
+
+    outs = []
+    for n, (a, b) in enumerate(((w, w_h), (m, m_h), (v, v_h))):
+        outs.append(pltpu.make_async_copy(a, b, t_s.at[n]))
+    for dc in range(2):
+        for p in range(4):
+            for j in range(nz):
+                at = lax.rem(z + nz - 1 - j, nz) * 2 + flip(x, p & 1)
+                at = at * shard + (flip(c, dc) * 2 + flip(y, p >> 1)) * quarter
+                outs.append(
+                    pltpu.make_async_copy(
+                        ag.at[dc, p, j, pl.ds(0, quarter)],
+                        roll_h.at[pl.ds(pl.multiple_of(at, BLOCK), quarter)],
+                        o_s.at[(dc * 4 + p) * nz + j],
+                    )
+                )
+    for copy in outs:
+        copy.start()
+    keys = keys_ref[...]
     keys = keys.astype(BF16)
     for s in range(steps):
         fk_o[s] = keys[s * rows : (s + 1) * rows]
@@ -445,8 +498,9 @@
             )
     for s in range(steps):
         att_o[s] = jnp.concatenate(lines[s], axis=0).astype(BF16)
-    for copy in sends:
-        copy.wait_send()
+    for n, (a, b) in enumerate(((fk_o, fk_h), (att_o, att_h))):
+        outs.append(pltpu.make_async_copy(a, b, t_s.at[3 + n]))
+        outs[-1].start()
     for copy in outs:
         copy.wait()
 
@@ -461,39 +515,41 @@
     slots = key_cache.shape[1]
     qrows = queries.shape[2] // hd * steps
     tokens = tokens_x.shape[0]
-    half = hd // 2
-    freq = rope_theta ** (-jnp.arange(half, dtype=F32) * 2.0 / hd)
-    positions = cache_lengths[None, :] + jnp.arange(steps, dtype=jnp.int32)[:, None]
-    angle = positions.astype(F32).reshape(-1, 1) * freq
-    cosine, sine = jnp.cos(angle), jnp.sin(angle)
-    cosr = jnp.concatenate([cosine, cosine], axis=1)
-    sinr = jnp.concatenate([-sine, sine], axis=1)
     vm = pl.BlockSpec(memory_space=pltpu.VMEM)
     dma = pltpu.SemaphoreType.DMA
     shape = jax.ShapeDtypeStruct
-    return pl.pallas_call(
+    anyspace = pl.BlockSpec(memory_space=pltpu.HBM)
+    vmem = pltpu.VMEM
+    made = pl.pallas_call(
         functools.partial(step_kernel, nz),
         out_shape=(
             shape((shard, hd), F32), shape((shard, hd), F32), shape((shard, hd), F32),
-            shape((width, hd), BF16), shape(new_values.shape, BF16), shape(queries.shape, BF16),
+            shape((2, 4, nz, quarter + TAIL, hd), BF16),
+            shape((steps * rows, hd), F32),
+            shape((rows, qrows, hd), F32),
+            shape((rows, qrows, slots), F32),
+            shape((rows, qrows, hd), F32),
+            shape((rows, qrows, hd), F32),
+            shape(value_cache.shape, BF16),
+            shape(new_values.shape, BF16),
         ),
-        in_specs=[vm] * 10 + [pl.BlockSpec(memory_space=pltpu.SMEM)] + [vm] * 2,
-        out_specs=(vm, vm, vm, pl.BlockSpec(memory_space=pl.ANY), vm, vm),
+        in_specs=[anyspace] * 11,
+        out_specs=(vm,) * 11,
         scratch_shapes=[
-            pltpu.VMEM((2 * nz, tokens, shard // 2), BF16),
-            pltpu.VMEM((tokens, hd), BF16),
-            pltpu.VMEM((3, nz, quarter, hd), BF16),
-            pltpu.VMEM((3, nz, quarter, hd), BF16),
-            pltpu.VMEM((nz, quarter, hd), F32),
-            pltpu.VMEM((nz, quarter, hd), F32),
-            pltpu.VMEM((nz - 1, quarter, hd), BF16),
-            pltpu.VMEM((nz - 1, quarter, hd), BF16),
-            pltpu.VMEM((4, quarter, hd), F32),
-            pltpu.VMEM((2, 4, nz, quarter + TAIL, hd), BF16),
-            pltpu.VMEM((rows, qrows, hd), F32),
-            pltpu.VMEM((rows, qrows, slots), F32),
-            pltpu.VMEM((rows, qrows, hd), F32),
-            pltpu.VMEM((rows, qrows, hd), F32),
+            vmem(tokens_x.shape, BF16), vmem(cotangent.shape, BF16),
+            vmem((shard, hd), F32), vmem((shard, hd), F32), vmem((shard, hd), F32),
+            vmem(hidden_dec.shape, BF16), vmem((steps * rows, width), BF16),
+            vmem(queries.shape, BF16), vmem(key_cache.shape, BF16),
+            pltpu.SMEM(cache_lengths.shape, jnp.int32), dma((11,)),
+            vmem((2 * nz, tokens, shard // 2), BF16),
+            vmem((tokens, hd), BF16),
+            vmem((3, nz, quarter, hd), BF16),
+            vmem((3, nz, quarter, hd), BF16),
+            vmem((nz, quarter, hd), F32),
+            vmem((nz, quarter, hd), F32),
+            vmem((nz - 1, quarter, hd), BF16),
+            vmem((nz - 1, quarter, hd), BF16),
+            vmem((4, quarter, hd), F32),
             dma((2 * nz + 1,)), dma((2 * nz + 1,)),
             dma((3, nz)), dma((3, nz)),
             dma((nz - 1,)), dma((nz - 1,)),
@@ -501,17 +557,34 @@
             dma((nz - 1,)), dma((nz - 1,)),
             dma((3, nz)), dma((3, nz)),
             dma((4, nz)), dma((4, nz)),
-            dma((8 * nz,)),
         ],
         compiler_params=pltpu.CompilerParams(
             collective_id=0, has_side_effects=True, vmem_limit_bytes=40 * 1024 * 1024
         ),
         name="step",
     )(
-        tokens_x, cotangent, master_weight, first_moment, second_moment,
-        hidden_dec.reshape(steps * rows, width), queries, new_values,
-        key_cache, value_cache, cache_lengths, cosr, sinr,
-    )
+        *(
+            pltpu.with_memory_space_constraint(arg, pltpu.HBM)
+            for arg in (
+                tokens_x, cotangent, master_weight, first_moment, second_moment,
+                hidden_dec, queries, new_values, key_cache, value_cache, cache_lengths,
+            )
+        )
+    )
+    return pl.pallas_call(
+        functools.partial(finish_kernel, nz),
+        out_shape=(
+            shape((shard, hd), F32), shape((shard, hd), F32), shape((shard, hd), F32),
+            shape((width, hd), BF16), shape(new_values.shape, BF16), shape(queries.shape, BF16),
+        ),
+        in_specs=[vm] * 11,
+        out_specs=(anyspace,) * 6,
+        scratch_shapes=[
+            vmem(new_values.shape, BF16), vmem(queries.shape, BF16), dma((8 * nz,)), dma((5,)),
+        ],
+        compiler_params=pltpu.CompilerParams(vmem_limit_bytes=8 * 1024 * 1024),
+        name="finish",
+    )(*made)
 
 
 def body(parts, replicas, *args):

time: 62.5 us -> 46.9 us (0.75)
  local copies, waits for them, and re-layouts: 15.4 us -> 0 us
  Pallas kernels: 45 us -> 46.1 us
  other arithmetic: 0.86 us -> 0 us
    unnamed x26 -> x0, local copies, waits for them, and re-layouts: 14.4 us -> none
    pallas_call x0 -> x1, Pallas kernels: none -> 2.39 us  [fused(): pl.pallas_call(functools.partial(finish_kernel, nz), out_shape=(shape((sh...]
    pallas_call x1, Pallas kernels: 45 us -> 43.7 us  [fused(): pl.pallas_call(functools.partial(step_kernel, nz), out_shape=(shape((shar...]
    reshape x1 -> x0, local copies, waits for them, and re-layouts: 0.87 us -> none  [fused(): hidden_dec.reshape(steps * rows, width)]
    convert_element_type x1 -> x0, other arithmetic: 0.66 us -> none  [fused(): angle = positions.astype(F32).reshape(-1, 1) * freq]
where the time goes in v2:
time: 46.9 us; the launch traced here: 46.7 us
  Pallas kernels  46.1 us (98%)
  between operations  0.64 us (1%)
    pallas_call x1, Pallas kernels, fused(): pl.pallas_call(functools.partial(step_kernel, nz), out_shape=(shape((shar...  43.7 us
    pallas_call x1, Pallas kernels, fused(): pl.pallas_call(functools.partial(finish_kernel, nz), out_shape=(shape((sh...  2.39 us

profile of v2, /device:TPU:0, one launch (start us, length us, event | category | flops | bytes accessed | tf_op | source)
XLA Modules:
  0.0 46.7 jit_solution(9766553866563056207)
XLA Ops:
  0.6 43.7 %step.1 = (f32[1024,128]{1,0:T(8,128)S(1)}, f32[1024,128]{1,0:T(8,128)S(1)}, f32[1024,128]{1,0:T(8,128)S(1)}, bf16[2,4,4,272,128]{4,3,2,1,0:T(8,128)(2,1)S(1)}, ...) custom-call(bf16[128,8192]{1,0:T(8,128)(2,1)} %tok_h.1, ...), custom_call_target="tpu_custom_call" | custom-call | tf_op jit(solution)/shard_map/step/pallas_call | solution.py:523
  44.3 2.4 %finish.1 = (f32[1024,128]{1,0:T(8,128)}, f32[1024,128]{1,0:T(8,128)}, f32[1024,128]{1,0:T(8,128)}, bf16[8192,128]{1,0:T(8,128)(2,1)}, bf16[2,2,128]{2,1,0:T(2,128)(2,1)}, /*index=5*/bf16[2,2,1024]{2,1,0:T(2,128)(2,1)}) custom-call(f32[1024,128]{1,0:T(8,128)S(1)} %get-tuple-element.17.w, f32[1024,128]{1,0:T(8,128)S(1)} %get-tuple-element.18.m, ...), custom_call_target="tpu_custom_call" | custom-call | tf_op jit(solution)/shard_map/finish/pallas_call | solution.py:574

commit v3 on v2

--- a/solution.py
+++ b/solution.py
@@ -138,6 +138,7 @@
 MESH = pl.DeviceIdType.MESH
 F32 = jnp.float32
 BF16 = jnp.bfloat16
+ORDER = (3, 2, 1, 0)
 TAIL = 16
 
 
@@ -149,7 +150,7 @@
     nz, tok_h, cot_h, wt_h, mo_h, ve_h, hid_h, qr_h, nv_h, kc_h, vc_h, lens_h,
     w_o, m_o, v_o, ag, raw_o, qs, ex, mx, sm, vc, nv,
     tok, cot, wt, mo, ve, hid3, hid, qr, kc, lens, in_s,
-    sib, sibcot, rs_s, rs_r, keep_b, keep_own, z_s, z_r, g_q,
+    sib, sibcot, rs_s, rs_r, z_s, z_r, g_q,
     sib_ss, sib_rs, rs_ss, rs_rs, z_ss, z_rs, g_ss, g_rs,
     az_ss, az_rs, ap_ss, ap_rs, as_ss, as_rs,
 ):
@@ -168,9 +169,11 @@
     def flip(value, bit):
         return 1 - value if bit else value
 
-    def device(dz=0, dx=0, dy=0, dc=0):
-        zz = lax.rem(z + dz, nz) if dz else z
-        return {"fsdp": zz * 2 + flip(x, dx), "rep": flip(y, dy) * 2 + flip(c, dc)}
+    def zx(m):
+        return flip(lax.div(z, 2), m >> 1) * 2 + flip(lax.rem(z, 2), m & 1)
+
+    def device(m=0, dx=0, dy=0, dc=0):
+        return {"fsdp": zx(m) * 2 + flip(x, dx), "rep": flip(y, dy) * 2 + flip(c, dc)}
 
     def remote(src, dst, ss, rs, where):
         return pltpu.make_async_remote_copy(
@@ -179,10 +182,10 @@
         )
 
     sibling = device(dc=1)
-    xn, yn = device(dx=1), device(dy=1)
-    zpeer = [device(dz=1 + j) for j in range(nz - 1)]
+    xn, yn, diag = device(dx=1), device(dy=1), device(dx=1, dy=1)
+    zpeer = {1: device(m=1), 2: device(m=2)}
     barrier = pltpu.get_barrier_semaphore()
-    peers = [sibling, xn, yn] + zpeer
+    peers = [sibling, xn, yn, zpeer[1], zpeer[2], diag]
     for peer in peers:
         pl.semaphore_signal(barrier, inc=1, device_id=peer, device_id_type=MESH)
 
@@ -195,9 +198,78 @@
     ]
     for load in loads:
         load.start()
+    pl.semaphore_wait(barrier, len(peers))
+
+    def target(j):
+        return zx(ORDER[j])
+
+    sends = []
+
+    def go(copy):
+        copy.start()
+        sends.append(copy)
+        return copy
+
+    cot_in = go(remote(cot_h, sibcot, sib_ss.at[2 * nz], sib_rs.at[2 * nz], sibling))
+    sib_in = {}
+    for j in range(nz):
+        for dx in (1, 0):
+            k = 2 * j + dx
+            off = pl.multiple_of((target(j) * 2 + flip(x, dx)) * shard + (1 - c) * half, BLOCK)
+            sib_in[j, dx] = go(
+                remote(tok_h.at[:, pl.ds(off, half)], sib.at[k], sib_ss.at[k], sib_rs.at[k], sibling)
+            )
+    cot_in.wait_recv()
+    loads[0].wait()
+    loads[1].wait()
+
+    def part(j, dx, dy):
+        at = flip(y, dy) * quarter
+        off = pl.multiple_of((target(j) * 2 + flip(x, dx)) * shard + c * half + at, BLOCK)
+        at = pl.multiple_of(at, BLOCK)
+        return tdot(tok[:, pl.ds(off, quarter)], cot[...]) + tdot(
+            sib[2 * j + dx, :, pl.ds(at, quarter)], sibcot[...]
+        )
+
+    def first(j):
+        return (1, 0) if j % 2 == 0 else (0, 1)
+
+    rs_in = {}
+
+    def stage_a(j):
+        sib_in[j, 1].wait_recv()
+        for n, dx, dy, where in ((1, 1, 1, diag), (0, 1, 0, xn), (2, 0, 1, yn)):
+            if n == 2:
+                sib_in[j, 0].wait_recv()
+            rs_s[n, j] = part(j, dx, dy).astype(BF16)
+            rs_in[n, j] = go(
+                remote(rs_s.at[n, j], rs_r.at[n, j], rs_ss.at[n, j], rs_rs.at[n, j], where)
+            )
+
+    z_in = {}
+
+    def stage_z(j):
+        mine = part(j, 0, 0)
+        rs_in[0, j].wait_recv()
+        rs_in[1, j].wait_recv()
+        rs_in[2, j].wait_recv()
+        total = mine + rs_r[0, j].astype(F32) + rs_r[1, j].astype(F32) + rs_r[2, j].astype(F32)
+        if j == nz - 1:
+            return total
+        if ORDER[j] == 2:
+            z_in[0].wait_recv()
+            total = total + z_r[0].astype(F32)
+        z_s[j] = total.astype(BF16)
+        where = zpeer[2 if ORDER[j] == 2 else 1]
+        z_in[j] = go(remote(z_s.at[j], z_r.at[j], z_ss.at[j], z_rs.at[j], where))
+        return None
+
+    for j in range(nz):
+        stage_a(j)
+    for j in range(nz - 1):
+        stage_z(j)
     for load in loads[2:6]:
         load.wait()
-    hid[...] = jnp.concatenate([hid3[s].astype(F32) for s in range(steps)], axis=0).astype(BF16)
 
     scale = 1.0 / math.sqrt(hd)
     for i in range(rows):
@@ -218,6 +290,51 @@
         mx[i] = jnp.broadcast_to(top, mx.shape[1:])
         sm[i] = jnp.broadcast_to(jnp.sum(e, axis=1, keepdims=True), sm.shape[1:])
 
+    grad = stage_z(nz - 1)
+    for j in range(1, nz - 1):
+        z_in[j].wait_recv()
+        grad = grad + z_r[j].astype(F32)
+    g_q[0] = grad
+    g_in = {
+        1: go(remote(g_q.at[0], g_q.at[1], g_ss.at[1], g_rs.at[1], yn)),
+        2: go(remote(g_q.at[0], g_q.at[2], g_ss.at[2], g_rs.at[2], sibling)),
+    }
+
+    def update(gradient, dy, dc):
+        at = pl.ds(pl.multiple_of((flip(c, dc) * 2 + flip(y, dy)) * quarter, BLOCK), quarter)
+        new = adamw(wt[at, :], mo[at, :], ve[at, :], gradient)
+        w_o[at, :], m_o[at, :], v_o[at, :] = new
+        return new[0]
+
+    for load in loads[6:]:
+        load.wait()
+    fresh = update(grad, 0, 0)
+    def quantize(fresh, p):
+        row = lax.broadcasted_iota(jnp.int32, (TAIL, hd), 0)
+        tail = jnp.zeros((TAIL, hd), F32)
+        for b in range(blocks):
+            piece = fresh[b * BLOCK : (b + 1) * BLOCK]
+            peak = jnp.max(jnp.max(jnp.abs(piece), axis=0, keepdims=True), axis=1, keepdims=True)
+            peak = peak + peak_eps
+            ag[0, p, nz - 1, b * BLOCK : (b + 1) * BLOCK] = (piece / peak).astype(BF16)
+            rest = jnp.broadcast_to(peak, (TAIL, hd))
+            for k in range(3):
+                high = rest.astype(BF16).astype(F32)
+                tail = jnp.where(row == 3 * b + k, high, tail)
+                rest = rest - high
+        ag[0, p, nz - 1, quarter : quarter + TAIL] = tail.astype(BF16)
+
+    quantize(fresh, 0)
+    az_in = {}
+
+    def along(src, j, where):
+        az_in[j] = go(
+            remote(ag.at[0, 0, src], ag.at[0, 0, j], az_ss.at[j], az_rs.at[j], zpeer[where])
+        )
+
+    along(nz - 1, 1, 2)
+    along(nz - 1, 2, 1)
+    hid[...] = jnp.concatenate([hid3[s].astype(F32) for s in range(steps)], axis=0).astype(BF16)
     row = lax.broadcasted_iota(jnp.int32, (steps * rows, hd), 0)
     lane = lax.broadcasted_iota(jnp.int32, (steps * rows, hd), 1)
     position = row // rows
@@ -229,124 +346,11 @@
     sine = jnp.sin(angle)
     sinr = jnp.where(lane < hd // 2, -sine, sine)
 
-    pl.semaphore_wait(barrier, len(peers))
-
-    def target(j):
-        return lax.rem(z + 1 + j, nz)
-
-    sends = []
-
-    def go(copy):
-        copy.start()
-        sends.append(copy)
-        return copy
-
-    cot_in = go(remote(cot_h, sibcot, sib_ss.at[2 * nz], sib_rs.at[2 * nz], sibling))
-    sib_in = {}
-    for j in range(nz):
-        for dx in (1, 0):
-            k = 2 * j + dx
-            off = pl.multiple_of((target(j) * 2 + flip(x, dx)) * shard + (1 - c) * half, BLOCK)
-            sib_in[j, dx] = go(
-                remote(tok_h.at[:, pl.ds(off, half)], sib.at[k], sib_ss.at[k], sib_rs.at[k], sibling)
-            )
-    cot_in.wait_recv()
-    loads[0].wait()
-    loads[1].wait()
-
-    def part(j, dx, dy):
-        at = flip(y, dy) * quarter
-        off = pl.multiple_of((target(j) * 2 + flip(x, dx)) * shard + c * half + at, BLOCK)
-        at = pl.multiple_of(at, BLOCK)
-        return tdot(tok[:, pl.ds(off, quarter)], cot[...]) + tdot(
-            sib[2 * j + dx, :, pl.ds(at, quarter)], sibcot[...]
-        )
-
-    def first(j):
-        return (1, 0) if j % 2 == 0 else (0, 1)
-
-    rs_in = {}
-
-    def stage_a(j):
-        da = first(j)
-        near, far = (xn, yn) if j % 2 == 0 else (yn, xn)
-        sib_in[j, 1].wait_recv()
-        if j % 2:
-            sib_in[j, 0].wait_recv()
-        rs_s[1, j] = part(j, 1, 1).astype(BF16)
-        rs_in[1, j] = go(remote(rs_s.at[1, j], rs_r.at[1, j], rs_ss.at[1, j], rs_rs.at[1, j], near))
-        rs_s[0, j] = part(j, *da).astype(BF16)
-        rs_in[0, j] = go(remote(rs_s.at[0, j], rs_r.at[0, j], rs_ss.at[0, j], rs_rs.at[0, j], near))
-        if j % 2 == 0:
-            sib_in[j, 0].wait_recv()
-        keep_b[j] = part(j, da[1], da[0])
-        keep_own[j] = part(j, 0, 0)
-
-    def stage_b(j):
-        far = yn if j % 2 == 0 else xn
-        rs_in[1, j].wait_recv()
-        rs_s[2, j] = (keep_b[j] + rs_r[1, j].astype(F32)).astype(BF16)
-        rs_in[2, j] = go(remote(rs_s.at[2, j], rs_r.at[2, j], rs_ss.at[2, j], rs_rs.at[2, j], far))
-
-    z_in = {}
-
-    def stage_z(j):
-        rs_in[0, j].wait_recv()
-        rs_in[2, j].wait_recv()
-        total = keep_own[j] + rs_r[0, j].astype(F32) + rs_r[2, j].astype(F32)
-        if j == nz - 1:
-            return total
-        z_s[j] = total.astype(BF16)
-        z_in[j] = go(remote(z_s.at[j], z_r.at[j], z_ss.at[j], z_rs.at[j], zpeer[j]))
-        return None
-
-    for j in range(nz):
-        stage_a(j)
-    stage_b(0)
-    for j in range(1, nz):
-        stage_b(j)
-        stage_z(j - 1)
-    grad = stage_z(nz - 1)
-    for j in range(nz - 1):
-        z_in[j].wait_recv()
-        grad = grad + z_r[j].astype(F32)
-    g_q[0] = grad
-    g_in = {
-        2: go(remote(g_q.at[0], g_q.at[2], g_ss.at[2], g_rs.at[2], sibling)),
-    }
-
-    def update(gradient, dy, dc):
-        at = pl.ds(pl.multiple_of((flip(c, dc) * 2 + flip(y, dy)) * quarter, BLOCK), quarter)
-        new = adamw(wt[at, :], mo[at, :], ve[at, :], gradient)
-        w_o[at, :], m_o[at, :], v_o[at, :] = new
-        return new[0]
-
-    for load in loads[6:]:
-        load.wait()
-    fresh = update(grad, 0, 0)
-    row = lax.broadcasted_iota(jnp.int32, (TAIL, hd), 0)
-    tail = jnp.zeros((TAIL, hd), F32)
-    for b in range(blocks):
-        piece = fresh[b * BLOCK : (b + 1) * BLOCK]
-        peak = jnp.max(jnp.max(jnp.abs(piece), axis=0, keepdims=True), axis=1, keepdims=True)
-        peak = peak + peak_eps
-        ag[0, 0, nz - 1, b * BLOCK : (b + 1) * BLOCK] = (piece / peak).astype(BF16)
-        rest = jnp.broadcast_to(peak, (TAIL, hd))
-        for k in range(3):
-            high = rest.astype(BF16).astype(F32)
-            tail = jnp.where(row == 3 * b + k, high, tail)
-            rest = rest - high
-    ag[0, 0, nz - 1, quarter : quarter + TAIL] = tail.astype(BF16)
-
-    az_in = {
-        j: go(remote(ag.at[0, 0, nz - 1], ag.at[0, 0, j], az_ss.at[j], az_rs.at[j], zpeer[j]))
-        for j in range(nz - 1)
-    }
     raw = [jnp.zeros((steps * rows, hd), F32)]
     ap_in, as_in = {}, {}
 
     def place(dc, p, j):
-        shard_at = lax.rem(z + nz - 1 - j, nz) * 2 + flip(x, p & 1)
+        shard_at = zx(ORDER[j]) * 2 + flip(x, p & 1)
         return shard_at * shard + (flip(c, dc) * 2 + flip(y, p >> 1)) * quarter
 
     def project(dc, p, j):
@@ -373,19 +377,24 @@
     def spread(j):
         if j < nz - 1:
             az_in[j].wait_recv()
+        if j == 1:
+            along(1, 0, 1)
+        plane(0, 3, j, diag)
         plane(0, 1, j, xn)
-        plane(0, 2, j, yn)
+        if j != nz - 1:
+            plane(0, 2, j, yn)
         share(0, j)
         project(0, 0, j)
 
     def relay(j):
         ap_in[1, j].wait_recv()
-        if j == 0:
-            plane(1, 3, j, yn)
         share(1, j)
-        ap_in[2, j].wait_recv()
-        if j != 0:
-            plane(2, 3, j, xn)
+        if j != nz - 1:
+            ap_in[2, j].wait_recv()
+        else:
+            g_in[1].wait_recv()
+            g_in[3] = go(remote(g_q.at[1], g_q.at[3], g_ss.at[3], g_rs.at[3], sibling))
+            quantize(update(g_q[1], 1, 0), 2)
         share(2, j)
         project(0, 1, j)
         project(0, 2, j)
@@ -400,17 +409,13 @@
         project(1, p, j)
 
     spread(nz - 1)
-    g_in[1] = go(remote(g_q.at[0], g_q.at[1], g_ss.at[1], g_rs.at[1], yn))
     g_in[2].wait_recv()
     update(g_q[2], 0, 1)
-    order = [nz - 1] + list(range(nz - 1))
+    order = [3, 2, 1, 0]
     for i in range(1, nz):
         spread(order[i])
         relay(order[i - 1])
         cross(0, order[i - 1])
-    g_in[1].wait_recv()
-    g_in[3] = go(remote(g_q.at[1], g_q.at[3], g_ss.at[3], g_rs.at[3], sibling))
-    update(g_q[1], 1, 0)
     relay(order[-1])
     g_in[3].wait_recv()
     update(g_q[3], 1, 1)
@@ -444,13 +449,16 @@
     def flip(value, bit):
         return 1 - value if bit else value
 
+    def zx(mask):
+        return flip(lax.div(z, 2), mask >> 1) * 2 + flip(lax.rem(z, 2), mask & 1)
+
     outs = []
     for n, (a, b) in enumerate(((w, w_h), (m, m_h), (v, v_h))):
         outs.append(pltpu.make_async_copy(a, b, t_s.at[n]))
     for dc in range(2):
         for p in range(4):
             for j in range(nz):
-                at = lax.rem(z + nz - 1 - j, nz) * 2 + flip(x, p & 1)
+                at = zx(ORDER[j]) * 2 + flip(x, p & 1)
                 at = at * shard + (flip(c, dc) * 2 + flip(y, p >> 1)) * quarter
                 outs.append(
                     pltpu.make_async_copy(
@@ -545,8 +553,6 @@
             vmem((tokens, hd), BF16),
             vmem((3, nz, quarter, hd), BF16),
             vmem((3, nz, quarter, hd), BF16),
-            vmem((nz, quarter, hd), F32),
-            vmem((nz, quarter, hd), F32),
             vmem((nz - 1, quarter, hd), BF16),
             vmem((nz - 1, quarter, hd), BF16),
             vmem((4, quarter, hd), F32),
@@ -589,7 +595,7 @@
 
 def body(parts, replicas, *args):
     quarter, left = divmod(args[2].shape[0], 4)
-    fits = replicas == 4 and parts >= 4 and parts % 2 == 0 and left == 0 and quarter % BLOCK == 0
+    fits = replicas == 4 and parts == 2 * len(ORDER) and left == 0 and quarter % BLOCK == 0
     if fits and quarter // BLOCK * 3 <= TAIL:
         return fused(parts // 2, *args)
     return shards(*args)

time: 46.9 us -> 44 us (0.938)
  Pallas kernels: 46.1 us -> 43.2 us
    pallas_call x1, Pallas kernels: 43.7 us -> 40.8 us  [fused(): pl.pallas_call(functools.partial(step_kernel, nz), out_shape=(shape((shar...]
where the time goes in v3:
time: 44 us; the launch traced here: 43.8 us
  Pallas kernels  43.2 us (98%)
  between operations  0.64 us (1%)
    pallas_call x1, Pallas kernels, fused(): pl.pallas_call(functools.partial(step_kernel, nz), out_shape=(shape((shar...  40.8 us
    pallas_call x1, Pallas kernels, fused(): pl.pallas_call(functools.partial(finish_kernel, nz), out_shape=(shape((sh...  2.39 us

profile of v3, /device:TPU:0, one launch (start us, length us, event | category | flops | bytes accessed | tf_op | source)
XLA Modules:
  0.0 43.8 jit_solution(6747687035075828955)
XLA Ops:
  0.6 40.8 %step.1 = (f32[1024,128]{1,0:T(8,128)S(1)}, f32[1024,128]{1,0:T(8,128)S(1)}, f32[1024,128]{1,0:T(8,128)S(1)}, bf16[2,4,4,272,128]{4,3,2,1,0:T(8,128)(2,1)S(1)}, ...) custom-call(bf16[128,8192]{1,0:T(8,128)(2,1)} %tok_h.1, ...), custom_call_target="tpu_custom_call" | custom-call | tf_op jit(solution)/shard_map/step/pallas_call | solution.py:531
  41.4 2.4 %finish.1 = (f32[1024,128]{1,0:T(8,128)}, f32[1024,128]{1,0:T(8,128)}, f32[1024,128]{1,0:T(8,128)}, bf16[8192,128]{1,0:T(8,128)(2,1)}, bf16[2,2,128]{2,1,0:T(2,128)(2,1)}, /*index=5*/bf16[2,2,1024]{2,1,0:T(2,128)(2,1)}) custom-call(f32[1024,128]{1,0:T(8,128)S(1)} %get-tuple-element.17.w, f32[1024,128]{1,0:T(8,128)S(1)} %get-tuple-element.18.m, ...), custom_call_target="tpu_custom_call" | custom-call | tf_op jit(solution)/shard_map/finish/pallas_call | solution.py:580
